TPU v7x, 32 devices: a whole 2x2x4 slice. The times are simulated.
32 devices in a mesh: dom: 8 (over z, y), group: 4 (over x, core).
Axes of the slice: x: 2, y: 2, z: 4, core: 2. Of those that a mesh axis runs over, the one named last changes fastest.
Arguments:
- features: bfloat16 [4096, 1024], P(('dom', 'group')), may hold values from -6 to 6
- out_grad: bfloat16 [4096, 1024], P(('dom', 'group')), may hold values from -0.1796875 to 0.1796875
- gcn_weight: bfloat16 [1024, 1024], replicated, may hold values from -0.1875 to 0.1875
- tile_index: int32 [32, 4], P(('dom', 'group')), may hold values from 0 to 2
- tile_edges: int32 [32, 4, 128, 128], P(('dom', 'group')), may hold values 0 or 1
- halo_rows: int32 [8, 4, 8, 32], P('dom', 'group'), may hold values from 0 to 127
- routes: int32 [4096, 2], P(('dom', 'group')), may hold values from 0 to 15, all different within a row; in each aligned block of 128 rows (0 to 127, 128 to 255, ...) at most 20 rows name the same one
- route_weight: float32 [4096, 2], P(('dom', 'group')), may hold values from 0.25 to 1
- up_weight: bfloat16 [16, 1024, 4096], P('dom', None, 'group'), may hold values from -0.1875 to 0.1875
- down_weight: bfloat16 [16, 4096, 1024], P('dom', 'group'), may hold values from -0.09375 to 0.09375
Outputs:
- node_out: bfloat16 [4096, 1024], P(('dom', 'group'))
- up_grad: bfloat16 [16, 1024, 4096], P('dom', None, 'group')
- down_grad: bfloat16 [16, 4096, 1024], P('dom', 'group')
Inputs may be any that keep to these rules, and one draw needn't show every extreme that they name: `routes`: in the rows of one partition no expert is named more than 20 times, and in every draw some partition names some expert exactly 20 times.
All inputs are finite; a program needn't handle non-finite values. No bound on the sum of `tile_edges` on one device may be relied on, other than what follows from the above.
Results may differ from a plain program's by a relative error of at most 0.0071.
Values may be sent and summed in bfloat16 or wider, within the bound.
A program may use at most 128 MiB of HBM per device.

v0:
```python
import jax
import jax.numpy as jnp
from jax import lax
from jax.sharding import PartitionSpec as P


def silu_slope(values):
    logistic = jax.nn.sigmoid(values)
    return logistic * (1.0 + values * (1.0 - logistic))


def slot_table(route_rows, expert_count, capacity):
    flat_ids = route_rows.reshape(-1)
    onehot = (flat_ids[:, None] == jnp.arange(expert_count, dtype=jnp.int32)[None, :]).astype(
        jnp.int32
    )
    before = jnp.cumsum(onehot, axis=0) - onehot
    within = jnp.sum(before * onehot, axis=1)
    target = flat_ids * capacity + within
    filler = (
        jnp.zeros((expert_count * capacity,), jnp.int32)
        .at[target]
        .set(jnp.arange(flat_ids.shape[0], dtype=jnp.int32) + 1)
    )
    return (target, filler)


def local(
    features,
    out_grad,
    gcn_weight,
    tile_index,
    tile_edges,
    halo_rows,
    routes,
    route_weight,
    up_weight,
    down_weight,
):
    dom_count = lax.axis_size("dom")
    group_count = lax.axis_size("group")
    node_count, width = features.shape
    tile_rows = tile_edges.shape[-1]
    local_tiles = tile_index.shape[0]
    border_rows = halo_rows.shape[-1]
    expert_local = up_weight.shape[0]
    expert_count = expert_local * dom_count
    top_count = routes.shape[1]
    capacity = max(2, 5 * node_count * top_count // (4 * expert_count))
    send_lists = halo_rows.reshape(-1)
    outgoing = features[send_lists].reshape(dom_count, border_rows, width)
    incoming = lax.all_to_all(outgoing, "dom", split_axis=0, concat_axis=0, tiled=True)
    sources = jnp.concatenate(
        [features, incoming.reshape(dom_count * border_rows, width)], axis=0
    ).reshape(-1, tile_rows, width)
    chosen = sources[tile_index]
    edge_values = tile_edges.astype(jnp.bfloat16)
    summed = features.reshape(local_tiles, tile_rows, width).astype(jnp.float32) + jnp.einsum(
        "tsij,tsjd->tid", edge_values, chosen, preferred_element_type=jnp.float32
    )
    degree = 1.0 + jnp.sum(tile_edges, axis=(1, 3)).astype(jnp.float32)
    aggregated = (
        (summed / jnp.sqrt(degree)[:, :, None]).reshape(node_count, width).astype(jnp.bfloat16)
    )
    preact = jnp.dot(aggregated, gcn_weight, preferred_element_type=jnp.float32)
    hidden = (features.astype(jnp.float32) + jax.nn.silu(preact)).astype(jnp.bfloat16)
    targets, fillers = slot_table(routes, expert_count, capacity)
    cotangent = (
        (route_weight[:, :, None] * out_grad[:, None, :].astype(jnp.float32))
        .astype(jnp.bfloat16)
        .reshape(-1, width)
    )
    present = (fillers > 0)[:, None]
    source_pair = jnp.maximum(fillers - 1, 0)
    nothing = jnp.zeros((), jnp.bfloat16)
    slot_shape = (dom_count, expert_local * capacity, width)
    send_hidden = jnp.where(present, hidden[source_pair // top_count], nothing).reshape(slot_shape)
    send_cot = jnp.where(present, cotangent[source_pair], nothing).reshape(slot_shape)
    mine_cot = lax.all_to_all(send_cot, "dom", split_axis=0, concat_axis=0, tiled=True)
    token_cot = lax.all_gather(mine_cot[None], "group", axis=0, tiled=True)
    mine_hidden = lax.all_to_all(send_hidden, "dom", split_axis=0, concat_axis=0, tiled=True)
    token_hidden = lax.all_gather(mine_hidden[None], "group", axis=0, tiled=True)
    sender_count = group_count * dom_count
    token_hidden = token_hidden.reshape(sender_count, expert_local, capacity, width)
    token_cot = token_cot.reshape(sender_count, expert_local, capacity, width)
    up_proj = jnp.einsum(
        "secd,edf->secf", token_hidden, up_weight, preferred_element_type=jnp.float32
    )
    active = jax.nn.silu(up_proj).astype(jnp.bfloat16)
    merged = lax.psum_scatter(
        jnp.einsum(
            "secf,efd->secd", active, down_weight, preferred_element_type=jnp.float32
        ).astype(jnp.bfloat16),
        "group",
        scatter_dimension=0,
        tiled=True,
    )
    expert_out = merged.reshape(dom_count, expert_local * capacity, width)
    returned = lax.all_to_all(expert_out, "dom", split_axis=0, concat_axis=0, tiled=True).reshape(
        expert_count * capacity, width
    )
    gathered = returned[targets].reshape(node_count, top_count, width)
    node_out = (
        hidden.astype(jnp.float32)
        + jnp.sum(route_weight[:, :, None] * gathered.astype(jnp.float32), axis=1)
    ).astype(jnp.bfloat16)
    grad_act = jnp.einsum(
        "secd,efd->secf", token_cot, down_weight, preferred_element_type=jnp.float32
    )
    grad_pre = (grad_act * silu_slope(up_proj)).astype(jnp.bfloat16)
    down_grad = jnp.einsum(
        "secf,secd->efd", active, token_cot, preferred_element_type=jnp.float32
    ).astype(jnp.bfloat16)
    up_grad = jnp.einsum(
        "secd,secf->edf", token_hidden, grad_pre, preferred_element_type=jnp.float32
    ).astype(jnp.bfloat16)
    return (node_out, up_grad, down_grad)


def solution(mesh):
    in_specs = (
        P(("dom", "group"), None),
        P(("dom", "group"), None),
        P(),
        P(("dom", "group"), None),
        P(("dom", "group"), None, None, None),
        P("dom", "group", None, None),
        P(("dom", "group"), None),
        P(("dom", "group"), None),
        P("dom", None, "group"),
        P("dom", "group", None),
    )
    out_specs = (P(("dom", "group"), None), P("dom", None, "group"), P("dom", "group", None))
    return jax.shard_map(local, mesh=mesh, in_specs=in_specs, out_specs=out_specs, check_vma=False)
```

profile of v0, /device:TPU:0, one launch (start us, length us, event | category | flops | bytes accessed | tf_op | source)
XLA Modules:
  0.0 192.9 jit_solution(4663778561806008242)
XLA Ops:
  8.2 3.3 %gather_fusion = bf16[256,1024]{1,0:T(8,128)(2,1)} fusion(bf16[128,1024]{1,0:T(8,128)(2,1)} %param.10, s32[1024]{0:T(1024)S(1)} %pad_clamp_fusion.4), kind=kCustom, calls=%fused_computation | custom fusion | bytes 1049600 | tf_op jit(solution)/shard_map/gather | solution.py:51
  11.5 7.3 %all-to-all-start = ((bf16[8,32,1024]{2,1,0:T(8,128)(2,1)}), bf16[8,32,1024]{2,1,0:T(8,128)(2,1)}, u32[]{:S(2)}, u32[]{:S(2)}) async-start(bf16[8,32,1024]{2,1,0:T(8,128)(2,1)} %bitcast.1), calls=%async_computation | async-start | bytes 1048576 | tf_op jit(solution)/shard_map/all_to_all | solution.py:52
  28.4 2.6 %gather_fusion.4 = bf16[320,1024]{1,0:T(8,128)(2,1)} fusion(bf16[256,1024]{1,0:T(8,128)(2,1)S(1)} %multiply_convert_fusion, s32[1024]{0:T(1024)S(1)} %get-tuple-element.16), kind=kCustom, calls=%fused_computation.4 | custom fusion | bytes 1312000 | tf_op jit(solution)/shard_map/gather | solution.py:78
  31.1 2.3 %all-to-all-done = bf16[8,32,1024]{2,1,0:T(8,128)(2,1)} async-done(((bf16[8,32,1024]{2,1,0:T(8,128)(2,1)}), bf16[8,32,1024]{2,1,0:T(8,128)(2,1)}, u32[]{:S(2)}, u32[]{:S(2)}) %all-to-all-start) | async-done | bytes 524320 | tf_op jit(solution)/shard_map/all_to_all | solution.py:52
  36.1 2.9 %fusion.24 = bf16[128,1024]{0,1:T(8,128)(2,1)S(1)} fusion(bf16[128,1024]{0,1:T(8,128)(2,1)} %copy.56, bf16[1024,1024]{1,0:T(8,128)(2,1)S(1)} %copy-done, bf16[4,128,1024]{2,1,0:T(8,128)(2,1)} %gather_fusion.1, f32[128]{0:T(128)S(1)} %add_sqrt_fusion, s32[1,4,128,128]{3,2,1,0:T(8,128)S(1)} %copy-done.6), kind=kOutput, calls=%fused_computation.38 | convolution fusion | flops 404160512 | bytes 3932672 | tf_op jit(solution)/shard_map/dot_general | solution.py:65
  39.1 2.6 %gather_fusion.2 = bf16[320,1024]{1,0:T(8,128)(2,1)} fusion(bf16[128,1024]{1,0:T(8,128)(2,1)S(1)} %copy.65, s32[1024]{0:T(1024)S(1)} %get-tuple-element.17), kind=kCustom, calls=%fused_computation.2 | custom fusion | bytes 1312000 | tf_op jit(solution)/shard_map/gather | solution.py:77
  43.0 21.4 %all_to_all.20 = bf16[8,40,1024]{2,1,0:T(8,128)(2,1)} all-to-all(bf16[8,40,1024]{2,1,0:T(8,128)(2,1)S(1)} %get-tuple-element.15), channel_id=1, replica_groups=mesh['dom'=8,'group'=4] {'dom'}, dimensions={0} | all-to-all | bytes 1310720 | tf_op jit(solution)/shard_map/all_to_all | solution.py:81
  64.5 20.7 %all_to_all.21 = bf16[8,40,1024]{2,1,0:T(8,128)(2,1)} all-to-all(bf16[8,40,1024]{2,1,0:T(8,128)(2,1)S(1)} %get-tuple-element.14), channel_id=1, replica_groups=mesh['dom'=8,'group'=4] {'dom'}, dimensions={0} | all-to-all | bytes 1310720 | tf_op jit(solution)/shard_map/all_to_all | solution.py:79
  85.4 3.4 %all-gather.5.cloned.1.call-done = bf16[32,40,1024]{2,1,0:T(8,128)(2,1)} async-done(((bf16[8,40,1024]{2,1,0:T(8,128)(2,1)}), bf16[32,40,1024]{2,1,0:T(8,128)(2,1)}) %all-gather.5.cloned.1.call-update) | async-done | bytes 2621456 | tf_op jit(solution)/shard_map/all_gather | solution.py:82
  88.8 3.3 %copy.66 = bf16[32,40,1024]{2,0,1:T(8,128)(2,1)S(1)} copy(bf16[32,40,1024]{2,1,0:T(8,128)(2,1)} %all-gather.5.cloned.1.call-done) | data formatting | bytes 5242880 | tf_op jit(solution)/shard_map/all_gather | solution.py:82
  93.7 2.9 %fusion.7 = f32[2,32,20,1024]{3,1,2,0:T(8,128)S(1)} fusion(bf16[32,2,20,1024]{3,0,2,1:T(8,128)(2,1)S(1)} %bitcast.122, bf16[2,1024,1024]{2,1,0:T(8,128)(2,1)S(1)} %copy-done.9), kind=kOutput, calls=%fused_computation.19 | convolution fusion | flops 2684354560 | bytes 12058624 | tf_op jit(solution)/shard_map/secd,edf->secf/dot_general | solution.py:86
  96.6 3.1 %convert_bitcast_fusion = bf16[32,2,20,1024]{3,0,2,1:T(8,128)(2,1)S(1)} fusion(bf16[2,1024,1024]{2,1,0:T(8,128)(2,1)S(1)} %copy-done.10, f32[2,32,20,1024]{3,1,2,0:T(8,128)S(1)} %fusion.7), kind=kOutput, calls=%fused_computation.25 | convolution fusion | flops 2692218880 | bytes 12058624 | tf_op jit(solution)/shard_map/secf,efd->secd/dot_general | solution.py:91
  99.8 3.1 %copy.78 = bf16[32,2,20,1024]{3,2,1,0:T(8,128)(2,1)} copy(bf16[32,2,20,1024]{3,0,2,1:T(8,128)(2,1)S(1)} %convert_bitcast_fusion) | data formatting | bytes 5242880
  102.9 4.9 %reshape.226 = bf16[32,40960]{1,0:T(8,128)(2,1)} reshape(bf16[32,2,20,1024]{3,2,1,0:T(8,128)(2,1)} %copy.78) | data formatting | bytes 5242880
  107.9 8.1 %all-gather.7.cloned.1.call-done = bf16[32,40,1024]{2,1,0:T(8,128)(2,1)} async-done(((bf16[8,40,1024]{2,1,0:T(8,128)(2,1)}), bf16[32,40,1024]{2,1,0:T(8,128)(2,1)}) %all-gather.7.cloned.1.call-update) | async-done | bytes 2621456 | tf_op jit(solution)/shard_map/all_gather | solution.py:80
  116.0 4.7 %copy.70 = bf16[32,40,1024]{2,0,1:T(8,128)(2,1)} copy(bf16[32,40,1024]{2,1,0:T(8,128)(2,1)} %all-gather.7.cloned.1.call-done) | data formatting | bytes 5242880 | tf_op jit(solution)/shard_map/all_gather | solution.py:80
  120.7 12.2 %bitcast_convert_fusion.1 = bf16[2,1024,1024]{2,1,0:T(8,128)(2,1)} fusion(bf16[32,2,20,1024]{3,0,2,1:T(8,128)(2,1)} %bitcast.123, f32[2,32,20,1024]{3,1,2,0:T(8,128)} %copy-done.12, bf16[32,2,20,1024]{3,0,2,1:T(8,128)(2,1)} %bitcast.124, bf16[2,1024,1024]{2,1,0:T(8,128)(2,1)} %param.19), kind=kOutput, calls=%fused_computation.7 | convolution fusion | flops 5382602752 | bytes 18874368 | tf_op jit(solution)/shard_map/secd,secf->edf/dot_general | solution.py:114
  132.9 20.3 %reduce-scatter.4.cloned.1.call-done = bf16[8,40960]{1,0:T(8,128)(2,1)} async-done(((bf16[32,40960]{1,0:T(8,128)(2,1)}), bf16[8,40960]{1,0:T(8,128)(2,1)}) %reduce-scatter.4.cloned.1.call-update) | async-done | bytes 655376
  153.2 2.3 %copy.67 = bf16[8,40,1024]{2,1,0:T(8,128)(2,1)} copy(bf16[8,40,1024]{2,0,1:T(8,128)(2,1)} %bitcast.128) | data formatting | bytes 1310720 | tf_op jit(solution)/shard_map/reshape | solution.py:98
  155.6 5.5 %all-to-all-start.2 = ((bf16[8,40,1024]{2,1,0:T(8,128)(2,1)}), bf16[8,40,1024]{2,1,0:T(8,128)(2,1)S(1)}, u32[]{:S(2)}, u32[]{:S(2)}) async-start(bf16[8,40,1024]{2,1,0:T(8,128)(2,1)} %copy.67), calls=%async_computation.2 | async-start | bytes 1310720 | tf_op jit(solution)/shard_map/all_to_all | solution.py:99
  161.1 8.9 %bitcast_convert_fusion = bf16[2,1024,1024]{2,1,0:T(8,128)(2,1)} fusion(bf16[32,2,20,1024]{3,0,2,1:T(8,128)(2,1)} %bitcast.125, f32[2,32,20,1024]{3,1,2,0:T(8,128)} %copy-done.12), kind=kOutput, calls=%fused_computation.6 | convolution fusion | flops 2693005312 | bytes 12058624 | tf_op jit(solution)/shard_map/secf,secd->efd/dot_general | solution.py:111
  169.9 8.4 %all-to-all-done.2 = bf16[8,40,1024]{2,1,0:T(8,128)(2,1)S(1)} async-done(((bf16[8,40,1024]{2,1,0:T(8,128)(2,1)}), bf16[8,40,1024]{2,1,0:T(8,128)(2,1)S(1)}, u32[]{:S(2)}, u32[]{:S(2)}) %all-to-all-start.2) | async-done | bytes 655392 | tf_op jit(solution)/shard_map/all_to_all | solution.py:99
  178.4 2.0 %gather_fusion.3 = bf16[256,1024]{1,0:T(8,128)(2,1)} fusion(bf16[320,1024]{1,0:T(8,128)(2,1)S(1)} %bitcast.120, s32[1024]{0:T(1024)S(1)} %pad_clamp_fusion.1), kind=kCustom, calls=%fused_computation.3 | custom fusion | bytes 1049600 | tf_op jit(solution)/shard_map/gather | solution.py:102
  182.0 2.1 %multiply_reduce_fusion = f32[128,1024]{1,0:T(8,128)} fusion(f32[128,2,1024]{2,1,0:T(2,128)S(1)} %reshape.164, f32[128,2]{1,0:T(8,128)S(1)} %copy.60), kind=kLoop, calls=%fused_computation.32 | loop fusion | flops 393216 | bytes 1573888 | tf_op jit(solution)/shard_map/reduce_sum | solution.py:105
  (73 shorter events, 20.3 us)
Async XLA Ops:
  7.2 28.9 %copy-start = (bf16[1024,1024]{1,0:T(8,128)(2,1)S(1)}, bf16[1024,1024]{1,0:T(8,128)(2,1)}, u32[]{:S(2)}) copy-start(bf16[1024,1024]{1,0:T(8,128)(2,1)} %param.12) | copy-start | bytes 6291460
  7.2 14.7 %copy-start.1 = (bf16[128,1024]{1,0:T(8,128)(2,1)S(1)}, bf16[128,1024]{1,0:T(8,128)(2,1)}, u32[]{:S(2)}) copy-start(bf16[128,1024]{1,0:T(8,128)(2,1)} %param.10) | copy-start | bytes 786436
  7.2 11.6 %copy-start.7 = (s32[128,2]{0,1:T(2,128)S(1)}, s32[128,2]{0,1:T(2,128)}, u32[]{:S(2)}) copy-start(s32[128,2]{0,1:T(2,128)} %param.16) | copy-start | bytes 3076
  8.1 17.5 %copy-start.8 = (f32[128,2]{0,1:T(2,128)S(1)}, f32[128,2]{0,1:T(2,128)}, u32[]{:S(2)}) copy-start(f32[128,2]{0,1:T(2,128)} %param.17) | copy-start | bytes 3076
  11.5 21.9 %all-to-all-start = ((bf16[8,32,1024]{2,1,0:T(8,128)(2,1)}), bf16[8,32,1024]{2,1,0:T(8,128)(2,1)}, u32[]{:S(2)}, u32[]{:S(2)}) async-start(bf16[8,32,1024]{2,1,0:T(8,128)(2,1)} %bitcast.1), calls=%async_computation | async-start | bytes 1048576 | tf_op jit(solution)/shard_map/all_to_all | solution.py:52
  18.8 70.0 %all-gather.5.cloned.1.call-start = ((), (), s32[]{:S(2)}) async-start(), calls=%async_computation.5 | async-start | bytes 3276800 | tf_op jit(solution)/shard_map/all_gather | solution.py:82
  25.6 5.4 %copy-start.11 = (s32[1,4]{1,0:T(1,128)S(1)}, s32[1,4]{1,0:T(1,128)}, u32[]{:S(2)}) copy-start(s32[1,4]{1,0:T(1,128)} %param.13) | copy-start | bytes 52
  28.4 7.6 %copy-start.6 = (s32[1,4,128,128]{3,2,1,0:T(8,128)S(1)}, s32[1,4,128,128]{3,2,1,0:T(8,128)}, u32[]{:S(2)}) copy-start(s32[1,4,128,128]{3,2,1,0:T(8,128)} %param.14) | copy-start | bytes 786436
  38.9 2.8 %copy-start.4 = (bf16[128,1024]{0,1:T(8,128)(2,1)}, bf16[128,1024]{0,1:T(8,128)(2,1)S(1)}, u32[]{:S(2)}) copy-start(bf16[128,1024]{0,1:T(8,128)(2,1)S(1)} %fusion.24) | copy-start | bytes 786436
  38.9 2.8 %copy-start.3 = (bf16[320,1024]{1,0:T(8,128)(2,1)S(1)}, bf16[320,1024]{1,0:T(8,128)(2,1)}, u32[]{:S(2)}) copy-start(bf16[320,1024]{1,0:T(8,128)(2,1)} %gather_fusion.4) | copy-start | bytes 1966084
  64.4 51.5 %all-gather.7.cloned.1.call-start = ((), (), s32[]{:S(2)}) async-start(), calls=%async_computation.6 | async-start | bytes 3276800 | tf_op jit(solution)/shard_map/all_gather | solution.py:80
  85.2 68.0 %reduce-scatter.4.cloned.1.call-start = ((), (), s32[]{:S(2)}) async-start(), calls=%async_computation.7 | async-start | bytes 3276800
  88.8 4.9 %copy-start.9 = (bf16[2,1024,1024]{2,1,0:T(8,128)(2,1)S(1)}, bf16[2,1024,1024]{2,1,0:T(8,128)(2,1)}, u32[]{:S(2)}) copy-start(bf16[2,1024,1024]{2,1,0:T(8,128)(2,1)} %param.18) | copy-start | bytes 12582916
  92.1 1.5 copy-start.2
  93.7 2.9 %copy-start.10 = (bf16[2,1024,1024]{2,1,0:T(8,128)(2,1)S(1)}, bf16[2,1024,1024]{2,1,0:T(8,128)(2,1)}, u32[]{:S(2)}) copy-start(bf16[2,1024,1024]{2,1,0:T(8,128)(2,1)} %param.19) | copy-start | bytes 12582916
  96.6 3.2 %copy-start.12 = (f32[2,32,20,1024]{3,1,2,0:T(8,128)}, f32[2,32,20,1024]{3,1,2,0:T(8,128)S(1)}, u32[]{:S(2)}) copy-start(f32[2,32,20,1024]{3,1,2,0:T(8,128)S(1)} %fusion.7) | copy-start | bytes 15728644
  155.6 22.8 %all-to-all-start.2 = ((bf16[8,40,1024]{2,1,0:T(8,128)(2,1)}), bf16[8,40,1024]{2,1,0:T(8,128)(2,1)S(1)}, u32[]{:S(2)}, u32[]{:S(2)}) async-start(bf16[8,40,1024]{2,1,0:T(8,128)(2,1)} %copy.67), calls=%async_computation.2 | async-start | bytes 1310720 | tf_op jit(solution)/shard_map/all_to_all | solution.py:99
  178.4 7.0 %copy-start.5 = (bf16[128,1024]{0,1:T(8,128)(2,1)S(1)}, bf16[128,1024]{0,1:T(8,128)(2,1)}, u32[]{:S(2)}) copy-start(bf16[128,1024]{0,1:T(8,128)(2,1)} %copy-done.4) | copy-start | bytes 786436
Sparse Core Ops, SparseCore 0:
  64.5 24.2 all-gather.4
  90.4 25.5 all-gather.6
  118.5 34.6 reduce-scatter.3
where the time goes:
time: 194 us; the launch traced here: 193 us
  local copies, waits for them, and re-layouts  43.4 us (22%)
  waiting for transfers between devices  42.6 us (22%)
  blocking collectives  42.1 us (22%)
  matrix products  30 us (15%)
  between operations  14 us (7%)
  starting transfers between devices  13.1 us (7%)
  other arithmetic  7.74 us (4%)
    all_to_all x1, blocking collectives, local(): lax.all_to_all(send_hidden, 'dom', split_axis=0, concat_axis=0, tiled=True)  21.4 us
    all_to_all x1, blocking collectives, local(): lax.all_to_all(send_cot, 'dom', split_axis=0, concat_axis=0, tiled=True)  20.7 us
    unnamed x4, waiting for transfers between devices  20.4 us
    dot_general x1, matrix products, local(): jnp.einsum('secd,secf->edf', token_hidden, grad_pre, preferred_element_ty...  12.2 us
    unnamed x32, local copies, waits for them, and re-layouts  11.6 us
    dot_general x1, matrix products, local(): jnp.einsum('secf,secd->efd', active, token_cot, preferred_element_type=jn...  8.86 us
    all_to_all x1, waiting for transfers between devices, local(): lax.all_to_all(expert_out, 'dom', split_axis=0, concat_axis=0, tiled=True)  8.44 us
    all_gather x1, waiting for transfers between devices, local(): token_cot = lax.all_gather(mine_cot[None], 'group', axis=0, tiled=True)  8.1 us
  transfers between devices with their start and end apart: 5, of which 5 were waited for; matrix products, arithmetic and copies ran while one was open for 29% of the time, Pallas kernels for 0%

commit v1 on v0

--- a/solution.py
+++ b/solution.py
@@ -2,6 +2,28 @@
 import jax.numpy as jnp
 from jax import lax
 from jax.sharding import PartitionSpec as P
+
+
+def split_up(shard, dim, peers):
+    before, after = (shard.shape[:dim], shard.shape[dim + 1 :])
+    return jnp.moveaxis(shard.reshape(*before, peers, -1, *after), dim, 0)
+
+
+def laid_out(blocks, dim):
+    blocks = jnp.moveaxis(blocks, 0, dim)
+    lengths = blocks.shape
+    return blocks.reshape(*lengths[:dim], lengths[dim] * lengths[dim + 1], *lengths[dim + 2 :])
+
+
+def pairwise_exchange(shard, axis, split_dim, concat_dim):
+    size, index = (lax.axis_size(axis), lax.axis_index(axis))
+    tiles = split_up(shard, split_dim, size)
+    outs = [tiles[index]]
+    for step in range(1, size):
+        sent = tiles[index ^ step]
+        outs.append(lax.ppermute(sent, axis, [(i, i ^ step) for i in range(size)]))
+    tiles = jnp.stack(outs)[index ^ jnp.arange(size)]
+    return laid_out(tiles, concat_dim)
 
 
 def silu_slope(values):
@@ -78,7 +100,7 @@
     send_cot = jnp.where(present, cotangent[source_pair], nothing).reshape(slot_shape)
     mine_cot = lax.all_to_all(send_cot, "dom", split_axis=0, concat_axis=0, tiled=True)
     token_cot = lax.all_gather(mine_cot[None], "group", axis=0, tiled=True)
-    mine_hidden = lax.all_to_all(send_hidden, "dom", split_axis=0, concat_axis=0, tiled=True)
+    mine_hidden = pairwise_exchange(send_hidden, "dom", 0, 0)
     token_hidden = lax.all_gather(mine_hidden[None], "group", axis=0, tiled=True)
     sender_count = group_count * dom_count
     token_hidden = token_hidden.reshape(sender_count, expert_local, capacity, width)

time: 194 us -> 196 us (1.010)
  blocking collectives: 42.1 us -> 21.8 us
  starting transfers between devices: 13.1 us -> 24.4 us
  waiting for transfers between devices: 42.6 us -> 52.6 us
    all_to_all x1 -> x0, blocking collectives: 21.4 us -> none  [local(): lax.all_to_all(send_hidden, 'dom', split_axis=0, concat_axis=0, tiled=True)]
    ppermute x0 -> x7, starting transfers between devices: none -> 11.3 us  [pairwise_exchange(): outs.append(lax.ppermute(sent, axis, [(i, i ^ step) for i in range(size)]))]
    all_to_all x1, waiting for transfers between devices: 2.26 us -> 11.9 us  [local(): lax.all_to_all(outgoing, 'dom', split_axis=0, concat_axis=0, tiled=True)]
    ppermute x0 -> x7, waiting for transfers between devices: none -> 6.9 us  [pairwise_exchange(): outs.append(lax.ppermute(sent, axis, [(i, i ^ step) for i in range(size)]))]
    all_gather x1, waiting for transfers between devices: 3.38 us -> 0.02 us  [local(): lax.all_gather(mine_hidden[None], 'group', axis=0, tiled=True)]
    all_gather x1, waiting for transfers between devices: 8.1 us -> 5.07 us  [local(): token_cot = lax.all_gather(mine_cot[None], 'group', axis=0, tiled=True)]
    unnamed x32 -> x36, local copies, waits for them, and re-layouts: 11.6 us -> 13.1 us
  transfers between devices with their start and end apart: 5 -> 12, of which waited for: 5 -> 6; matrix products, arithmetic and copies ran while one was open for 29% -> 27% of each run, Pallas kernels for 0% -> 0%
where the time goes in v1:
time: 196 us; the launch traced here: 195 us
  waiting for transfers between devices  52.6 us (27%)
  local copies, waits for them, and re-layouts  45.1 us (23%)
  matrix products  30.1 us (15%)
  starting transfers between devices  24.4 us (12%)
  blocking collectives  21.8 us (11%)
  between operations  14.2 us (7%)
  other arithmetic  6.63 us (3%)
    all_to_all x1, blocking collectives, local(): lax.all_to_all(send_cot, 'dom', split_axis=0, concat_axis=0, tiled=True)  21.8 us
    unnamed x4, waiting for transfers between devices  20.4 us
    unnamed x36, local copies, waits for them, and re-layouts  13.1 us
    dot_general x1, matrix products, local(): jnp.einsum('secd,secf->edf', token_hidden, grad_pre, preferred_element_ty...  12.2 us
    all_to_all x1, waiting for transfers between devices, local(): lax.all_to_all(outgoing, 'dom', split_axis=0, concat_axis=0, tiled=True)  11.9 us
    ppermute x7, starting transfers between devices, pairwise_exchange(): outs.append(lax.ppermute(sent, axis, [(i, i ^ step) for i in range(size)]))  11.3 us
    dot_general x1, matrix products, local(): jnp.einsum('secf,secd->efd', active, token_cot, preferred_element_type=jn...  8.86 us
    all_to_all x1, waiting for transfers between devices, local(): lax.all_to_all(expert_out, 'dom', split_axis=0, concat_axis=0, tiled=True)  8.44 us
  transfers between devices with their start and end apart: 12, of which 6 were waited for; matrix products, arithmetic and copies ran while one was open for 27% of the time, Pallas kernels for 0%

profile of v1, /device:TPU:0, one launch (start us, length us, event | category | flops | bytes accessed | tf_op | source)
XLA Modules:
  0.0 194.8 jit_solution(8032662026414236810)
XLA Ops:
  11.1 3.3 %gather_fusion = bf16[256,1024]{1,0:T(8,128)(2,1)} fusion(bf16[128,1024]{1,0:T(8,128)(2,1)} %param.10, s32[1024]{0:T(1024)S(1)} %pad_clamp_fusion.5), kind=kCustom, calls=%fused_computation | custom fusion | bytes 1049600 | tf_op jit(solution)/shard_map/gather | solution.py:73
  14.4 7.3 %all-to-all-start = ((bf16[8,32,1024]{2,1,0:T(8,128)(2,1)}), bf16[8,32,1024]{2,1,0:T(8,128)(2,1)S(1)}, u32[]{:S(2)}, u32[]{:S(2)}) async-start(bf16[8,32,1024]{2,1,0:T(8,128)(2,1)} %bitcast.1), calls=%async_computation | async-start | bytes 1048576 | tf_op jit(solution)/shard_map/all_to_all | solution.py:74
  24.3 11.9 %all-to-all-done = bf16[8,32,1024]{2,1,0:T(8,128)(2,1)S(1)} async-done(((bf16[8,32,1024]{2,1,0:T(8,128)(2,1)}), bf16[8,32,1024]{2,1,0:T(8,128)(2,1)S(1)}, u32[]{:S(2)}, u32[]{:S(2)}) %all-to-all-start) | async-done | bytes 524320 | tf_op jit(solution)/shard_map/all_to_all | solution.py:74
  39.7 3.0 %fusion.24 = bf16[128,1024]{0,1:T(8,128)(2,1)S(1)} fusion(bf16[128,1024]{0,1:T(8,128)(2,1)} %copy.56, bf16[1024,1024]{1,0:T(8,128)(2,1)S(1)} %copy-done, bf16[4,128,1024]{2,1,0:T(8,128)(2,1)} %gather_fusion.1, f32[128]{0:T(128)S(1)} %add_sqrt_fusion, s32[1,4,128,128]{3,2,1,0:T(8,128)} %param.14), kind=kOutput, calls=%fused_computation.39 | convolution fusion | flops 404160512 | bytes 3932672 | tf_op jit(solution)/shard_map/dot_general | solution.py:87
  42.8 2.1 %gather_fusion.2 = bf16[320,1024]{1,0:T(8,128)(2,1)S(1)} fusion(bf16[128,1024]{1,0:T(8,128)(2,1)S(1)} %copy.65, s32[1024]{0:T(1024)S(1)} %pad_clamp_fusion.3), kind=kCustom, calls=%fused_computation.2 | custom fusion | bytes 1312000 | tf_op jit(solution)/shard_map/gather | solution.py:99
  48.8 3.7 %collective-permute-start.4 = (bf16[1,40,1024]{2,1,0:T(8,128)(2,1)S(1)}, bf16[1,40,1024]{2,1,0:T(8,128)(2,1)S(1)}, u32[]{:S(2)}, u32[]{:S(2)}) collective-permute-start(bf16[1,40,1024]{2,1,0:T(8,128)(2,1)S(1)} %get-tuple-element.14), channel_id=1, source_target_pairs={{0,20},{4,16},{8,28},{12,24},{16,4},{20,0},{24,12},{28,8},{1,21},{... | collective-permute-start | bytes 245768 | tf_op jit(solution)/shard_map/ppermute | solution.py:24
  53.9 2.4 %collective-permute-start.6 = (bf16[1,40,1024]{2,1,0:T(8,128)(2,1)S(1)}, bf16[1,40,1024]{2,1,0:T(8,128)(2,1)S(1)}, u32[]{:S(2)}, u32[]{:S(2)}) collective-permute-start(bf16[1,40,1024]{2,1,0:T(8,128)(2,1)S(1)} %get-tuple-element.12), channel_id=1, source_target_pairs={{0,28},{4,24},{8,20},{12,16},{16,12},{20,8},{24,4},{28,0},{1,29},{... | collective-permute-start | bytes 245768 | tf_op jit(solution)/shard_map/ppermute | solution.py:24
  56.4 4.6 %collective-permute-done.3 = bf16[1,40,1024]{2,1,0:T(8,128)(2,1)S(1)} collective-permute-done((bf16[1,40,1024]{2,1,0:T(8,128)(2,1)S(1)}, bf16[1,40,1024]{2,1,0:T(8,128)(2,1)S(1)}, u32[]{:S(2)}, u32[]{:S(2)}) %collective-permute-start.3) | collective-permute-done | bytes 81952 | tf_op jit(solution)/shard_map/ppermute | solution.py:24
  61.0 2.3 %collective-permute-done.4 = bf16[1,40,1024]{2,1,0:T(8,128)(2,1)S(1)} collective-permute-done((bf16[1,40,1024]{2,1,0:T(8,128)(2,1)S(1)}, bf16[1,40,1024]{2,1,0:T(8,128)(2,1)S(1)}, u32[]{:S(2)}, u32[]{:S(2)}) %collective-permute-start.4) | collective-permute-done | bytes 81952 | tf_op jit(solution)/shard_map/ppermute | solution.py:24
  71.7 21.8 %all_to_all.15 = bf16[8,40,1024]{2,1,0:T(8,128)(2,1)} all-to-all(bf16[8,40,1024]{2,1,0:T(8,128)(2,1)S(1)} %broadcast_select_fusion), channel_id=1, replica_groups=mesh['dom'=8,'group'=4] {'dom'}, dimensions={0} | all-to-all | bytes 1310720 | tf_op jit(solution)/shard_map/all_to_all | solution.py:101
  93.8 3.3 %copy.66 = bf16[32,40,1024]{2,0,1:T(8,128)(2,1)S(1)} copy(bf16[32,40,1024]{2,1,0:T(8,128)(2,1)} %all-gather.5.cloned.1.call-done) | data formatting | bytes 5242880 | tf_op jit(solution)/shard_map/all_gather | solution.py:104
  98.7 2.9 %fusion.7 = f32[2,32,20,1024]{3,1,2,0:T(8,128)S(1)} fusion(bf16[32,2,20,1024]{3,0,2,1:T(8,128)(2,1)S(1)} %bitcast.153, bf16[2,1024,1024]{2,1,0:T(8,128)(2,1)S(1)} %copy-done.8), kind=kOutput, calls=%fused_computation.20 | convolution fusion | flops 2684354560 | bytes 12058624 | tf_op jit(solution)/shard_map/secd,edf->secf/dot_general | solution.py:108
  101.6 3.1 %convert_bitcast_fusion = bf16[32,2,20,1024]{3,0,2,1:T(8,128)(2,1)S(1)} fusion(bf16[2,1024,1024]{2,1,0:T(8,128)(2,1)S(1)} %copy-done.9, f32[2,32,20,1024]{3,1,2,0:T(8,128)S(1)} %fusion.7), kind=kOutput, calls=%fused_computation.26 | convolution fusion | flops 2692218880 | bytes 12058624 | tf_op jit(solution)/shard_map/secf,efd->secd/dot_general | solution.py:113
  104.7 3.1 %copy.78 = bf16[32,2,20,1024]{3,2,1,0:T(8,128)(2,1)} copy(bf16[32,2,20,1024]{3,0,2,1:T(8,128)(2,1)S(1)} %convert_bitcast_fusion) | data formatting | bytes 5242880
  107.8 4.9 %reshape.262 = bf16[32,40960]{1,0:T(8,128)(2,1)} reshape(bf16[32,2,20,1024]{3,2,1,0:T(8,128)(2,1)} %copy.78) | data formatting | bytes 5242880
  112.8 5.1 %all-gather.7.cloned.1.call-done = bf16[32,40,1024]{2,1,0:T(8,128)(2,1)} async-done(((bf16[8,40,1024]{2,1,0:T(8,128)(2,1)}), bf16[32,40,1024]{2,1,0:T(8,128)(2,1)}) %all-gather.7.cloned.1.call-update) | async-done | bytes 2621456 | tf_op jit(solution)/shard_map/all_gather | solution.py:102
  117.9 4.7 %copy.70 = bf16[32,40,1024]{2,0,1:T(8,128)(2,1)} copy(bf16[32,40,1024]{2,1,0:T(8,128)(2,1)} %all-gather.7.cloned.1.call-done) | data formatting | bytes 5242880 | tf_op jit(solution)/shard_map/all_gather | solution.py:102
  122.6 12.2 %bitcast_convert_fusion.1 = bf16[2,1024,1024]{2,1,0:T(8,128)(2,1)} fusion(bf16[32,2,20,1024]{3,0,2,1:T(8,128)(2,1)} %bitcast.154, f32[2,32,20,1024]{3,1,2,0:T(8,128)} %copy-done.11, bf16[32,2,20,1024]{3,0,2,1:T(8,128)(2,1)} %bitcast.155, bf16[2,1024,1024]{2,1,0:T(8,128)(2,1)} %param.19), kind=kOutput, calls=%fused_computation.8 | convolution fusion | flops 5382602752 | bytes 18874368 | tf_op jit(solution)/shard_map/secd,secf->edf/dot_general | solution.py:136
  134.8 20.3 %reduce-scatter.4.cloned.1.call-done = bf16[8,40960]{1,0:T(8,128)(2,1)} async-done(((bf16[32,40960]{1,0:T(8,128)(2,1)}), bf16[8,40960]{1,0:T(8,128)(2,1)}) %reduce-scatter.4.cloned.1.call-update) | async-done | bytes 655376
  155.1 2.3 %copy.67 = bf16[8,40,1024]{2,1,0:T(8,128)(2,1)} copy(bf16[8,40,1024]{2,0,1:T(8,128)(2,1)} %bitcast.161) | data formatting | bytes 1310720 | tf_op jit(solution)/shard_map/reshape | solution.py:120
  157.4 5.5 %all-to-all-start.1 = ((bf16[8,40,1024]{2,1,0:T(8,128)(2,1)}), bf16[8,40,1024]{2,1,0:T(8,128)(2,1)S(1)}, u32[]{:S(2)}, u32[]{:S(2)}) async-start(bf16[8,40,1024]{2,1,0:T(8,128)(2,1)} %copy.67), calls=%async_computation.1 | async-start | bytes 1310720 | tf_op jit(solution)/shard_map/all_to_all | solution.py:121
  162.9 8.9 %bitcast_convert_fusion = bf16[2,1024,1024]{2,1,0:T(8,128)(2,1)} fusion(bf16[32,2,20,1024]{3,0,2,1:T(8,128)(2,1)} %bitcast.156, f32[2,32,20,1024]{3,1,2,0:T(8,128)} %copy-done.11), kind=kOutput, calls=%fused_computation.7 | convolution fusion | flops 2693005312 | bytes 12058624 | tf_op jit(solution)/shard_map/secf,secd->efd/dot_general | solution.py:133
  171.8 8.4 %all-to-all-done.1 = bf16[8,40,1024]{2,1,0:T(8,128)(2,1)S(1)} async-done(((bf16[8,40,1024]{2,1,0:T(8,128)(2,1)}), bf16[8,40,1024]{2,1,0:T(8,128)(2,1)S(1)}, u32[]{:S(2)}, u32[]{:S(2)}) %all-to-all-start.1) | async-done | bytes 655392 | tf_op jit(solution)/shard_map/all_to_all | solution.py:121
  183.9 2.2 %multiply_reduce_fusion = f32[128,1024]{1,0:T(8,128)} fusion(f32[128,2,1024]{2,1,0:T(2,128)S(1)} %reshape.190, f32[128,2]{1,0:T(8,128)S(1)} %copy-done.5), kind=kLoop, calls=%fused_computation.33 | loop fusion | flops 393216 | bytes 1573888 | tf_op jit(solution)/shard_map/reduce_sum | solution.py:127
  (96 shorter events, 31.3 us)
Async XLA Ops:
  7.2 32.5 %copy-start = (bf16[1024,1024]{1,0:T(8,128)(2,1)S(1)}, bf16[1024,1024]{1,0:T(8,128)(2,1)}, u32[]{:S(2)}) copy-start(bf16[1024,1024]{1,0:T(8,128)(2,1)} %param.12) | copy-start | bytes 6291460
  7.2 16.0 %copy-start.1 = (bf16[128,1024]{1,0:T(8,128)(2,1)S(1)}, bf16[128,1024]{1,0:T(8,128)(2,1)}, u32[]{:S(2)}) copy-start(bf16[128,1024]{1,0:T(8,128)(2,1)} %param.10) | copy-start | bytes 786436
  7.2 16.9 %copy-start.6 = (s32[1,4,128,128]{3,2,1,0:T(8,128)S(1)}, s32[1,4,128,128]{3,2,1,0:T(8,128)}, u32[]{:S(2)}) copy-start(s32[1,4,128,128]{3,2,1,0:T(8,128)} %param.14) | copy-start | bytes 786436
  7.2 17.0 %copy-start.10 = (s32[1,4]{1,0:T(1,128)S(1)}, s32[1,4]{1,0:T(1,128)}, u32[]{:S(2)}) copy-start(s32[1,4]{1,0:T(1,128)} %param.13) | copy-start | bytes 52
  14.4 21.8 %all-to-all-start = ((bf16[8,32,1024]{2,1,0:T(8,128)(2,1)}), bf16[8,32,1024]{2,1,0:T(8,128)(2,1)S(1)}, u32[]{:S(2)}, u32[]{:S(2)}) async-start(bf16[8,32,1024]{2,1,0:T(8,128)(2,1)} %bitcast.1), calls=%async_computation | async-start | bytes 1048576 | tf_op jit(solution)/shard_map/all_to_all | solution.py:74
  21.7 72.1 %all-gather.5.cloned.1.call-start = ((), (), s32[]{:S(2)}) async-start(), calls=%async_computation.4 | async-start | bytes 3276800 | tf_op jit(solution)/shard_map/all_gather | solution.py:104
  36.2 0.8 copy-start.3
  44.9 20.0 %copy-start.7 = (f32[128,2]{0,1:T(2,128)S(1)}, f32[128,2]{0,1:T(2,128)}, u32[]{:S(2)}) copy-start(f32[128,2]{0,1:T(2,128)} %param.17) | copy-start | bytes 3076
  45.1 7.4 %collective-permute-start = (bf16[1,40,1024]{2,1,0:T(8,128)(2,1)S(1)}, bf16[1,40,1024]{2,1,0:T(8,128)(2,1)S(1)}, u32[]{:S(2)}, u32[]{:S(2)}) collective-permute-start(bf16[1,40,1024]{2,1,0:T(8,128)(2,1)S(1)} %get-tuple-element.18), channel_id=1, source_target_pairs={{0,4},{4,0},{8,12},{12,8},{16,20},{20,16},{24,28},{28,24},{1,5},{5... | collective-permute-start | bytes 245768 | tf_op jit(solution)/shard_map/ppermute | solution.py:24
  46.6 7.3 %collective-permute-start.1 = (bf16[1,40,1024]{2,1,0:T(8,128)(2,1)S(1)}, bf16[1,40,1024]{2,1,0:T(8,128)(2,1)S(1)}, u32[]{:S(2)}, u32[]{:S(2)}) collective-permute-start(bf16[1,40,1024]{2,1,0:T(8,128)(2,1)S(1)} %get-tuple-element.17), channel_id=1, source_target_pairs={{0,8},{4,12},{8,0},{12,4},{16,24},{20,28},{24,16},{28,20},{1,9},{5... | collective-permute-start | bytes 245768 | tf_op jit(solution)/shard_map/ppermute | solution.py:24
  46.6 9.8 %collective-permute-start.2 = (bf16[1,40,1024]{2,1,0:T(8,128)(2,1)S(1)}, bf16[1,40,1024]{2,1,0:T(8,128)(2,1)S(1)}, u32[]{:S(2)}, u32[]{:S(2)}) collective-permute-start(bf16[1,40,1024]{2,1,0:T(8,128)(2,1)S(1)} %get-tuple-element.16), channel_id=1, source_target_pairs={{0,12},{4,8},{8,4},{12,0},{16,28},{20,24},{24,20},{28,16},{1,13},{... | collective-permute-start | bytes 245768 | tf_op jit(solution)/shard_map/ppermute | solution.py:24
  48.6 12.3 %collective-permute-start.3 = (bf16[1,40,1024]{2,1,0:T(8,128)(2,1)S(1)}, bf16[1,40,1024]{2,1,0:T(8,128)(2,1)S(1)}, u32[]{:S(2)}, u32[]{:S(2)}) collective-permute-start(bf16[1,40,1024]{2,1,0:T(8,128)(2,1)S(1)} %get-tuple-element.15), channel_id=1, source_target_pairs={{0,16},{4,20},{8,24},{12,28},{16,0},{20,4},{24,8},{28,12},{1,17},{... | collective-permute-start | bytes 245768 | tf_op jit(solution)/shard_map/ppermute | solution.py:24
  48.8 14.5 %collective-permute-start.4 = (bf16[1,40,1024]{2,1,0:T(8,128)(2,1)S(1)}, bf16[1,40,1024]{2,1,0:T(8,128)(2,1)S(1)}, u32[]{:S(2)}, u32[]{:S(2)}) collective-permute-start(bf16[1,40,1024]{2,1,0:T(8,128)(2,1)S(1)} %get-tuple-element.14), channel_id=1, source_target_pairs={{0,20},{4,16},{8,28},{12,24},{16,4},{20,0},{24,12},{28,8},{1,21},{... | collective-permute-start | bytes 245768 | tf_op jit(solution)/shard_map/ppermute | solution.py:24
  52.5 10.8 %collective-permute-start.5 = (bf16[1,40,1024]{2,1,0:T(8,128)(2,1)S(1)}, bf16[1,40,1024]{2,1,0:T(8,128)(2,1)S(1)}, u32[]{:S(2)}, u32[]{:S(2)}) collective-permute-start(bf16[1,40,1024]{2,1,0:T(8,128)(2,1)S(1)} %get-tuple-element.13), channel_id=1, source_target_pairs={{0,24},{4,28},{8,16},{12,20},{16,8},{20,12},{24,0},{28,4},{1,25},{... | collective-permute-start | bytes 245768 | tf_op jit(solution)/shard_map/ppermute | solution.py:24
  53.9 9.4 %collective-permute-start.6 = (bf16[1,40,1024]{2,1,0:T(8,128)(2,1)S(1)}, bf16[1,40,1024]{2,1,0:T(8,128)(2,1)S(1)}, u32[]{:S(2)}, u32[]{:S(2)}) collective-permute-start(bf16[1,40,1024]{2,1,0:T(8,128)(2,1)S(1)} %get-tuple-element.12), channel_id=1, source_target_pairs={{0,28},{4,24},{8,20},{12,16},{16,12},{20,8},{24,4},{28,0},{1,29},{... | collective-permute-start | bytes 245768 | tf_op jit(solution)/shard_map/ppermute | solution.py:24
  64.8 53.1 %all-gather.7.cloned.1.call-start = ((), (), s32[]{:S(2)}) async-start(), calls=%async_computation.5 | async-start | bytes 3276800 | tf_op jit(solution)/shard_map/all_gather | solution.py:102
  65.0 3.1 %copy-start.4 = (f32[128,2]{1,0:T(8,128)}, f32[128,2]{1,0:T(8,128)S(1)}, u32[]{:S(2)}) copy-start(f32[128,2]{1,0:T(8,128)S(1)} %copy.60) | copy-start | bytes 3076
  93.5 61.6 %reduce-scatter.4.cloned.1.call-start = ((), (), s32[]{:S(2)}) async-start(), calls=%async_computation.6 | async-start | bytes 3276800
  93.8 4.9 %copy-start.8 = (bf16[2,1024,1024]{2,1,0:T(8,128)(2,1)S(1)}, bf16[2,1024,1024]{2,1,0:T(8,128)(2,1)}, u32[]{:S(2)}) copy-start(bf16[2,1024,1024]{2,1,0:T(8,128)(2,1)} %param.18) | copy-start | bytes 12582916
  97.1 1.6 copy-start.2
  98.7 2.9 %copy-start.9 = (bf16[2,1024,1024]{2,1,0:T(8,128)(2,1)S(1)}, bf16[2,1024,1024]{2,1,0:T(8,128)(2,1)}, u32[]{:S(2)}) copy-start(bf16[2,1024,1024]{2,1,0:T(8,128)(2,1)} %param.19) | copy-start | bytes 12582916
  101.6 3.1 %copy-start.11 = (f32[2,32,20,1024]{3,1,2,0:T(8,128)}, f32[2,32,20,1024]{3,1,2,0:T(8,128)S(1)}, u32[]{:S(2)}) copy-start(f32[2,32,20,1024]{3,1,2,0:T(8,128)S(1)} %fusion.7) | copy-start | bytes 15728644
  157.4 22.8 %all-to-all-start.1 = ((bf16[8,40,1024]{2,1,0:T(8,128)(2,1)}), bf16[8,40,1024]{2,1,0:T(8,128)(2,1)S(1)}, u32[]{:S(2)}, u32[]{:S(2)}) async-start(bf16[8,40,1024]{2,1,0:T(8,128)(2,1)} %copy.67), calls=%async_computation.1 | async-start | bytes 1310720 | tf_op jit(solution)/shard_map/all_to_all | solution.py:121
  171.8 12.1 %copy-start.5 = (f32[128,2]{1,0:T(8,128)S(1)}, f32[128,2]{1,0:T(8,128)}, u32[]{:S(2)}) copy-start(f32[128,2]{1,0:T(8,128)} %copy-done.4) | copy-start | bytes 3076
Sparse Core Ops, SparseCore 0:
  64.9 25.7 all-gather.4
  93.6 24.1 all-gather.6
  120.4 34.6 reduce-scatter.3
